TPU v7x, 512 devices: a whole 4x8x8 slice. The times are simulated.
512 devices in a mesh: snap: 32 (over x_hi, y, core), var: 16 (over z, x_lo).
Axes of the slice: x: 4 (x_hi: 2, x_lo: 2; x = x_hi * 2 + x_lo), y: 8, z: 8, core: 2. Of those that a mesh axis runs over, the one named last changes fastest.
Arguments:
- tensor: float32 [512, 1280, 1024], P('var', 'snap'), may hold values from 0.05 to 5
- cell_factor: float32 [1024, 256], P('snap'), may hold values from 0.1 to 1
- var_factor: float32 [512, 256], P('var'), may hold values from 0.1 to 1
- snap_factor: float32 [1280, 256], P('snap'), may hold values from 0.002 to 0.02
Outputs:
- grad_cells: float32 [1024, 256], P('snap')
- grad_vars: float32 [512, 256], P('var')
- grad_snaps: float32 [1280, 256], P('snap')
All inputs are finite; a program needn't handle non-finite values.
Results may differ from a plain program's by a relative error of at most 0.0003.
Values sent between devices are 32-bit elements; how exact they have to be, the bound alone decides.
No kernel may reach another device: no remote copies, remote signals or barrier semaphores. Data moves between devices by JAX's collectives and lax.ppermute only.
A program may use at most 64 MiB of HBM per device.

v0:
```python
import jax
import jax.numpy as jnp
from jax import lax
from jax.sharding import PartitionSpec as P

high = lax.Precision.HIGHEST


def local(tensor, cell_factor, var_factor, snap_factor):
    var_rows, snap_rows, cells = tensor.shape
    rank = cell_factor.shape[1]
    khatri = (var_factor[:, None, :] * snap_factor[None, :, :]).reshape(var_rows * snap_rows, rank)
    flat = tensor.reshape(var_rows * snap_rows, cells)
    all_cells = lax.all_gather(cell_factor, "snap", axis=0, tiled=True)
    model = jnp.dot(khatri, all_cells.T, precision=high, preferred_element_type=jnp.float32)
    deriv = (model - flat) * lax.rsqrt(model)
    partial_cells = jnp.dot(deriv.T, khatri, precision=high, preferred_element_type=jnp.float32)
    folded = jnp.dot(deriv, all_cells, precision=high, preferred_element_type=jnp.float32).reshape(
        var_rows, snap_rows, rank
    )
    partial_vars = jnp.einsum("vsr,sr->vr", folded, snap_factor, precision=high)
    partial_snaps = jnp.einsum("vsr,vr->sr", folded, var_factor, precision=high)
    summed = lax.psum(partial_cells, "var")
    grad_cells = lax.psum_scatter(summed, "snap", scatter_dimension=0, tiled=True)
    grad_vars = lax.psum(partial_vars, "snap")
    grad_snaps = lax.psum(partial_snaps, "var")
    return (grad_cells, grad_vars, grad_snaps)


def solution(mesh):
    placed = (P("var", "snap", None), P("snap", None), P("var", None), P("snap", None))
    return jax.shard_map(
        local,
        mesh=mesh,
        in_specs=placed,
        out_specs=(P("snap", None), P("var", None), P("snap", None)),
        check_vma=False,
    )
```

profile of v0, /device:TPU:6, one launch (start us, length us, event | category | flops | bytes accessed | tf_op | source)
XLA Modules:
  0.0 389.5 jit_solution(5850247747479945227)
XLA Ops:
  7.2 0.0 all-gather.2.cloned.1.call-start
  7.2 0.7 all-gather.2.cloned.1.call-update
  7.9 0.0 reduce-scatter.2.cloned.1.call-start
  7.9 0.9 broadcast_multiply_fusion
  8.8 88.6 %all-gather.2.cloned.1.call-done = f32[1024,256]{1,0:T(8,128)} async-done(((f32[32,256]{1,0:T(8,128)}), f32[1024,256]{1,0:T(8,128)}) %all-gather.2.cloned.1.call-update) | async-done | bytes 1048592 | tf_op jit(solution)/shard_map/all_gather | solution.py:14
  97.4 6.9 %fusion = f32[1280,1024]{1,0:T(8,128)S(1)} fusion(f32[32,40,1024]{2,1,0:T(8,128)} %param.4, f32[1280,256]{1,0:T(8,128)S(1)} %bitcast.20, f32[1024,256]{1,0:T(8,128)} %all-gather.2.cloned.1.call-done), kind=kOutput, calls=%fused_computation.1 | convolution fusion | flops 4029153280 | bytes 12845056 | tf_op jit(solution)/shard_map/dot_general | solution.py:15
  104.4 2.3 copy-done
  106.7 9.6 %fusion.1 = f32[1024,256]{1,0:T(8,128)} fusion(f32[1280,1024]{1,0:T(8,128)S(1)} %fusion, f32[1280,256]{1,0:T(8,128)S(1)} %bitcast.21), kind=kOutput, calls=%fused_computation.5 | convolution fusion | flops 4026531840 | bytes 7602176 | tf_op jit(solution)/shard_map/dot_general | solution.py:17
  116.2 0.0 reduce-scatter.2.cloned.1.call-update
  116.3 0.0 copy-start.3
  116.3 0.2 all-reduce.3.cloned.1.call-start
  116.5 1.0 copy-done.1
  117.5 6.2 %fusion.2 = f32[1280,256]{1,0:T(8,128)S(1)} fusion(f32[1280,1024]{1,0:T(8,128)} %copy-done, f32[1024,256]{1,0:T(8,128)S(1)} %copy-done.1), kind=kOutput, calls=%fused_computation.6 | convolution fusion | flops 4026531840 | bytes 7602176 | tf_op jit(solution)/shard_map/dot_general | solution.py:18
  123.7 0.0 copy-start.2
  123.7 0.0 copy-done.3
  123.7 0.7 multiply_reduce_fusion
  124.4 113.6 %reduce-scatter.2.cloned.1.call-done = f32[32,256]{1,0:T(8,128)} async-done(((f32[1024,256]{1,0:T(8,128)}), f32[32,256]{1,0:T(8,128)}) %reduce-scatter.2.cloned.1.call-update) | async-done | bytes 32784 | tf_op jit(solution)/shard_map/reduce_scatter | solution.py:24
  238.0 0.0 all-reduce.3.cloned.1.call-update
  238.1 0.0 copy-done.2
  238.1 0.1 multiply_reduce_fusion.1
  238.2 129.1 %psum.22 = f32[32,256]{1,0:T(8,128)} all-reduce(f32[32,256]{1,0:T(8,128)S(1)} %bitcast.27), channel_id=1, replica_groups=mesh['snap'=32,'var'=16] {'snap'}, use_global_device_ids=true, to_apply=%region_2.0 | all-reduce | flops 8192 | bytes 65536 | tf_op jit(solution)/shard_map/psum | solution.py:25
  367.3 12.8 %all-reduce.3.cloned.1.call-done = (f32[32,256]{1,0:T(8,128)}, f32[40,256]{1,0:T(8,128)}) async-done(((f32[32,256]{1,0:T(8,128)}, f32[40,256]{1,0:T(8,128)}), (f32[32,256]{1,0:T(8,128)}, f32[40,256]{1,0:T(8,128)})) %all-reduce.3.cloned.1.call-update) | async-done | bytes 73744 | tf_op jit(solution)/shard_map/psum | solution.py:23
  380.2 1.4 copy.23
  381.5 1.4 copy.24
  (2 shorter events, 0.0 us)
Async XLA Ops:
  7.2 90.3 %all-gather.2.cloned.1.call-start = ((), (), s32[]{:S(2)}) async-start(), calls=%async_computation.1 | async-start | bytes 1081344 | tf_op jit(solution)/shard_map/all_gather | solution.py:14
  7.9 230.1 %reduce-scatter.2.cloned.1.call-start = ((), (), s32[]{:S(2)}) async-start(), calls=%async_computation.2 | async-start | bytes 1081344 | tf_op jit(solution)/shard_map/reduce_scatter | solution.py:24
  104.4 2.3 copy-start
  116.2 1.2 copy-start.1
  116.3 7.4 %copy-start.3 = (f32[32,256]{1,0:T(8,128)S(1)}, f32[32,256]{1,0:T(8,128)}, u32[]{:S(2)}) copy-start(f32[32,256]{1,0:T(8,128)} %param.6) | copy-start | bytes 98308
  116.3 263.9 %all-reduce.3.cloned.1.call-start = ((), (), s32[]{:S(2)}) async-start(), calls=%async_computation.3 | async-start | bytes 147456 | tf_op jit(solution)/shard_map/psum | solution.py:23
  123.7 114.4 %copy-start.2 = (f32[40,256]{1,0:T(8,128)S(1)}, f32[40,256]{1,0:T(8,128)}, u32[]{:S(2)}) copy-start(f32[40,256]{1,0:T(8,128)} %param.7) | copy-start | bytes 122884
Sparse Core Ops, SparseCore 0:
  11.3 86.0 all-gather.1
  116.4 121.6 reduce-scatter.1
  241.6 138.5 all-reduce.2
where the time goes:
time: 390 us; the launch traced here: 389 us
  waiting for transfers between devices  216 us (55%)
  blocking collectives  129 us (33%)
  matrix products  22.7 us (6%)
  between operations  13.8 us (4%)
  local copies, waits for them, and re-layouts  6.04 us (2%)
    psum x1, blocking collectives, local(): grad_vars = lax.psum(partial_vars, 'snap')  129 us
    reduce_scatter x1, waiting for transfers between devices, local(): lax.psum_scatter(summed, 'snap', scatter_dimension=0, tiled=True)  114 us
    all_gather x1, waiting for transfers between devices, local(): all_cells = lax.all_gather(cell_factor, 'snap', axis=0, tiled=True)  88.6 us
    psum x1, waiting for transfers between devices, local(): summed = lax.psum(partial_cells, 'var')  12.8 us
    dot_general x1, matrix products, local(): jnp.dot(deriv.T, khatri, precision=high, preferred_element_type=jnp.float32)  9.55 us
  transfers between devices with their start and end apart: 3, of which 3 were waited for; matrix products, arithmetic and copies ran while one was open for 2% of the time, Pallas kernels for 0%

commit v1 on v0

--- a/solution.py
+++ b/solution.py
@@ -22,7 +22,7 @@
     partial_snaps = jnp.einsum("vsr,vr->sr", folded, var_factor, precision=high)
     summed = lax.psum(partial_cells, "var")
     grad_cells = lax.psum_scatter(summed, "snap", scatter_dimension=0, tiled=True)
-    grad_vars = lax.psum(partial_vars, "snap")
+    grad_vars = jnp.sum(lax.all_gather(partial_vars, "snap"), axis=0)
     grad_snaps = lax.psum(partial_snaps, "var")
     return (grad_cells, grad_vars, grad_snaps)
 

time: 390 us -> 474 us (1.22)
  waiting for transfers between devices: 216 us -> 426 us
  blocking collectives: 129 us -> 0 us
    psum x1 -> x0, blocking collectives: 129 us -> none  [local(): grad_vars = lax.psum(partial_vars, 'snap')]
    psum x1, waiting for transfers between devices: 12.8 us -> 139 us  [local(): summed = lax.psum(partial_cells, 'var')]
    all_gather x0 -> x1, waiting for transfers between devices: none -> 85.1 us  [local(): grad_vars = jnp.sum(lax.all_gather(partial_vars, 'snap'), axis=0)]
  transfers between devices with their start and end apart: 3 -> 4, of which waited for: 3 -> 4; matrix products, arithmetic and copies ran while one was open for 2% -> 2% of each run, Pallas kernels for 0% -> 0%
where the time goes in v1:
time: 474 us; the launch traced here: 473 us
  waiting for transfers between devices  426 us (90%)
  matrix products  22.7 us (5%)
  between operations  13.8 us (3%)
  local copies, waits for them, and re-layouts  6.03 us (1%)
    psum x1, waiting for transfers between devices, local(): summed = lax.psum(partial_cells, 'var')  139 us
    reduce_scatter x1, waiting for transfers between devices, local(): lax.psum_scatter(summed, 'snap', scatter_dimension=0, tiled=True)  113 us
    all_gather x1, waiting for transfers between devices, local(): all_cells = lax.all_gather(cell_factor, 'snap', axis=0, tiled=True)  88.6 us
    all_gather x1, waiting for transfers between devices, local(): grad_vars = jnp.sum(lax.all_gather(partial_vars, 'snap'), axis=0)  85.1 us
    dot_general x1, matrix products, local(): jnp.dot(deriv.T, khatri, precision=high, preferred_element_type=jnp.float32)  9.55 us
  transfers between devices with their start and end apart: 4, of which 4 were waited for; matrix products, arithmetic and copies ran while one was open for 2% of the time, Pallas kernels for 0%

profile of v1, /device:TPU:6, one launch (start us, length us, event | category | flops | bytes accessed | tf_op | source)
XLA Modules:
  0.0 473.4 jit_solution(3849814898418604008)
XLA Ops:
  7.2 0.0 all-gather.4.cloned.1.call-start
  7.2 0.7 all-gather.4.cloned.1.call-update
  7.9 0.0 reduce-scatter.2.cloned.1.call-start
  7.9 0.9 broadcast_multiply_fusion
  8.8 88.6 %all-gather.4.cloned.1.call-done = f32[1024,256]{1,0:T(8,128)} async-done(((f32[32,256]{1,0:T(8,128)}), f32[1024,256]{1,0:T(8,128)}) %all-gather.4.cloned.1.call-update) | async-done | bytes 1048592 | tf_op jit(solution)/shard_map/all_gather | solution.py:14
  97.4 6.9 %fusion = f32[1280,1024]{1,0:T(8,128)S(1)} fusion(f32[32,40,1024]{2,1,0:T(8,128)} %param.4, f32[1280,256]{1,0:T(8,128)S(1)} %bitcast.21, f32[1024,256]{1,0:T(8,128)} %all-gather.4.cloned.1.call-done), kind=kOutput, calls=%fused_computation.1 | convolution fusion | flops 4029153280 | bytes 12845056 | tf_op jit(solution)/shard_map/dot_general | solution.py:15
  104.4 2.3 copy-done
  106.7 9.6 %fusion.1 = f32[1024,256]{1,0:T(8,128)} fusion(f32[1280,1024]{1,0:T(8,128)S(1)} %fusion, f32[1280,256]{1,0:T(8,128)S(1)} %bitcast.22), kind=kOutput, calls=%fused_computation.5 | convolution fusion | flops 4026531840 | bytes 7602176 | tf_op jit(solution)/shard_map/dot_general | solution.py:17
  116.2 0.0 reduce-scatter.2.cloned.1.call-update
  116.2 0.0 copy-start.2
  116.3 0.2 all-gather.6.cloned.1.call-start
  116.5 1.0 copy-done.1
  117.4 6.2 %fusion.2 = f32[1280,256]{1,0:T(8,128)S(1)} fusion(f32[1280,1024]{1,0:T(8,128)} %copy-done, f32[1024,256]{1,0:T(8,128)S(1)} %copy-done.1), kind=kOutput, calls=%fused_computation.6 | convolution fusion | flops 4026531840 | bytes 7602176 | tf_op jit(solution)/shard_map/dot_general | solution.py:18
  123.7 0.8 multiply_reduce_fusion.1
  124.4 0.0 all-gather.6.cloned.1.call-update
  124.4 0.0 all-reduce.3.cloned.1.call-start
  124.5 0.7 multiply_reduce_fusion
  125.3 112.8 %reduce-scatter.2.cloned.1.call-done = f32[32,256]{1,0:T(8,128)} async-done(((f32[1024,256]{1,0:T(8,128)}), f32[32,256]{1,0:T(8,128)}) %reduce-scatter.2.cloned.1.call-update) | async-done | bytes 32784 | tf_op jit(solution)/shard_map/reduce_scatter | solution.py:24
  238.0 0.0 all-reduce.3.cloned.1.call-update
  238.0 85.1 %all-gather.6.cloned.1.call-done = f32[1024,256]{1,0:T(8,128)} async-done(((f32[32,256]{1,0:T(8,128)}), f32[1024,256]{1,0:T(8,128)}) %all-gather.6.cloned.1.call-update) | async-done | bytes 1048592 | tf_op jit(solution)/shard_map/all_gather | solution.py:25
  323.2 1.9 reduce_sum.9
  325.1 139.0 %all-reduce.3.cloned.1.call-done = (f32[32,256]{1,0:T(8,128)}, f32[40,256]{1,0:T(8,128)}) async-done(((f32[32,256]{1,0:T(8,128)}, f32[40,256]{1,0:T(8,128)}), (f32[32,256]{1,0:T(8,128)}, f32[40,256]{1,0:T(8,128)})) %all-reduce.3.cloned.1.call-update) | async-done | bytes 73744 | tf_op jit(solution)/shard_map/psum | solution.py:23
  464.1 1.4 copy.23
  465.5 1.4 copy.24
  (5 shorter events, 0.0 us)
Async XLA Ops:
  7.2 90.3 %all-gather.4.cloned.1.call-start = ((), (), s32[]{:S(2)}) async-start(), calls=%async_computation.1 | async-start | bytes 1081344 | tf_op jit(solution)/shard_map/all_gather | solution.py:14
  7.9 230.1 %reduce-scatter.2.cloned.1.call-start = ((), (), s32[]{:S(2)}) async-start(), calls=%async_computation.3 | async-start | bytes 1081344 | tf_op jit(solution)/shard_map/reduce_scatter | solution.py:24
  104.4 2.3 copy-start
  116.2 1.2 copy-start.1
  116.2 7.4 %copy-start.2 = (f32[40,256]{1,0:T(8,128)S(1)}, f32[40,256]{1,0:T(8,128)}, u32[]{:S(2)}) copy-start(f32[40,256]{1,0:T(8,128)} %param.7) | copy-start | bytes 122884
  116.3 206.9 %all-gather.6.cloned.1.call-start = ((), (), s32[]{:S(2)}) async-start(), calls=%async_computation.2 | async-start | bytes 1081344 | tf_op jit(solution)/shard_map/all_gather | solution.py:25
  123.6 0.9 copy-start.3
  124.4 339.6 %all-reduce.3.cloned.1.call-start = ((), (), s32[]{:S(2)}) async-start(), calls=%async_computation.4 | async-start | bytes 147456 | tf_op jit(solution)/shard_map/psum | solution.py:23
Sparse Core Ops, SparseCore 0:
  11.3 86.0 all-gather.3
  116.4 121.6 reduce-scatter.1
  242.0 81.1 all-gather.5
  326.6 137.4 all-reduce.2

commit v2 on v0

--- a/solution.py
+++ b/solution.py
@@ -11,7 +11,9 @@
     rank = cell_factor.shape[1]
     khatri = (var_factor[:, None, :] * snap_factor[None, :, :]).reshape(var_rows * snap_rows, rank)
     flat = tensor.reshape(var_rows * snap_rows, cells)
-    all_cells = lax.all_gather(cell_factor, "snap", axis=0, tiled=True)
+    all_cells = jnp.concatenate(
+        lax.all_to_all(jnp.stack([cell_factor] * lax.axis_size("snap")), "snap", 0, 0), axis=0
+    )
     model = jnp.dot(khatri, all_cells.T, precision=high, preferred_element_type=jnp.float32)
     deriv = (model - flat) * lax.rsqrt(model)
     partial_cells = jnp.dot(deriv.T, khatri, precision=high, preferred_element_type=jnp.float32)

time: 390 us -> 342 us (0.88)
  waiting for transfers between devices: 216 us -> 157 us
  starting transfers between devices: 0.3 us -> 10.6 us
    all_gather x1 -> x0, waiting for transfers between devices: 88.6 us -> none  [local(): all_cells = lax.all_gather(cell_factor, 'snap', axis=0, tiled=True)]
    all_to_all x0 -> x1, waiting for transfers between devices: none -> 27.2 us  [local(): lax.all_to_all(jnp.stack([cell_factor] * lax.axis_size('snap')), 'snap',...]
    all_to_all x0 -> x1, starting transfers between devices: none -> 10.4 us  [local(): lax.all_to_all(jnp.stack([cell_factor] * lax.axis_size('snap')), 'snap',...]
where the time goes in v2:
time: 342 us; the launch traced here: 341 us
  waiting for transfers between devices  157 us (46%)
  blocking collectives  129 us (38%)
  matrix products  23 us (7%)
  between operations  14.1 us (4%)
  starting transfers between devices  10.6 us (3%)
  local copies, waits for them, and re-layouts  6.95 us (2%)
    psum x1, blocking collectives, local(): grad_vars = lax.psum(partial_vars, 'snap')  129 us
    reduce_scatter x1, waiting for transfers between devices, local(): lax.psum_scatter(summed, 'snap', scatter_dimension=0, tiled=True)  117 us
    all_to_all x1, waiting for transfers between devices, local(): lax.all_to_all(jnp.stack([cell_factor] * lax.axis_size('snap')), 'snap',...  27.2 us
    psum x1, waiting for transfers between devices, local(): summed = lax.psum(partial_cells, 'var')  12.9 us
    all_to_all x1, starting transfers between devices, local(): lax.all_to_all(jnp.stack([cell_factor] * lax.axis_size('snap')), 'snap',...  10.4 us
    dot_general x1, matrix products, local(): jnp.dot(deriv.T, khatri, precision=high, preferred_element_type=jnp.float32)  9.57 us
  transfers between devices with their start and end apart: 3, of which 3 were waited for; matrix products, arithmetic and copies ran while one was open for 2% of the time, Pallas kernels for 0%

profile of v2, /device:TPU:6, one launch (start us, length us, event | category | flops | bytes accessed | tf_op | source)
XLA Modules:
  0.0 341.2 jit_solution(556202444231684559)
XLA Ops:
  7.2 1.9 stack.2
  9.0 0.0 copy-start.1
  9.0 0.0 copy-start.2
  9.0 10.4 %all-to-all-start = ((f32[32,32,256]{2,1,0:T(8,128)}), f32[32,32,256]{2,1,0:T(8,128)S(1)}, u32[]{:S(2)}, u32[]{:S(2)}) async-start(f32[32,32,256]{2,1,0:T(8,128)} %stack.2), calls=%async_computation | async-start | bytes 2097152 | tf_op jit(solution)/shard_map/all_to_all | solution.py:15
  19.4 0.0 reduce-scatter.2.cloned.1.call-start
  19.5 0.0 copy-done.1
  19.5 0.0 copy-done.2
  19.5 0.1 broadcast_multiply_fusion
  19.6 27.2 %all-to-all-done = f32[32,32,256]{2,1,0:T(8,128)S(1)} async-done(((f32[32,32,256]{2,1,0:T(8,128)}), f32[32,32,256]{2,1,0:T(8,128)S(1)}, u32[]{:S(2)}, u32[]{:S(2)}) %all-to-all-start) | async-done | bytes 1048608 | tf_op jit(solution)/shard_map/all_to_all | solution.py:15
  46.8 6.6 %fusion = f32[1280,1024]{1,0:T(8,128)S(1)} fusion(f32[32,40,1024]{2,1,0:T(8,128)} %param.4, f32[1280,256]{1,0:T(8,128)S(1)} %bitcast.24, f32[1024,256]{1,0:T(8,128)S(1)} %bitcast.26), kind=kOutput, calls=%fused_computation.1 | convolution fusion | flops 4029153280 | bytes 12845056 | tf_op jit(solution)/shard_map/dot_general | solution.py:17
  53.5 0.0 copy-start
  53.5 2.3 copy-done
  55.8 9.6 %fusion.1 = f32[1024,256]{1,0:T(8,128)} fusion(f32[1280,1024]{1,0:T(8,128)S(1)} %fusion, f32[1280,256]{1,0:T(8,128)S(1)} %bitcast.25), kind=kOutput, calls=%fused_computation.5 | convolution fusion | flops 4026531840 | bytes 7602176 | tf_op jit(solution)/shard_map/dot_general | solution.py:19
  65.3 0.0 reduce-scatter.2.cloned.1.call-update
  65.4 0.2 all-reduce.3.cloned.1.call-start
  65.6 6.8 %multiply_reduce_fusion = (f32[256,40]{0,1:T(8,128)}, f32[32,40,256]{2,1,0:T(8,128)S(1)}) fusion(f32[256,32]{0,1:T(8,128)S(1)} %bitcast.30, f32[32,40,1024]{2,1,0:T(8,128)} %bitcast.23, f32[1024,256,1]{1,0,2:T(8,128)S(1)} %bitcast.27), kind=kOutput, calls=%fused_computation.2 | convolution fusion | flops 4027176960 | bytes 7675904 | tf_op jit(solution)/shard_map/dot_general | solution.py:20
  72.4 117.0 %reduce-scatter.2.cloned.1.call-done = f32[32,256]{1,0:T(8,128)} async-done(((f32[1024,256]{1,0:T(8,128)}), f32[32,256]{1,0:T(8,128)}) %reduce-scatter.2.cloned.1.call-update) | async-done | bytes 32784 | tf_op jit(solution)/shard_map/reduce_scatter | solution.py:26
  189.4 0.0 all-reduce.3.cloned.1.call-update
  189.4 0.1 multiply_reduce_fusion.1
  189.6 129.1 %psum.22 = f32[32,256]{1,0:T(8,128)} all-reduce(f32[32,256]{1,0:T(8,128)S(1)} %bitcast.31), channel_id=1, replica_groups=mesh['snap'=32,'var'=16] {'snap'}, use_global_device_ids=true, to_apply=%region_2.0 | all-reduce | flops 8192 | bytes 65536 | tf_op jit(solution)/shard_map/psum | solution.py:27
  318.7 12.9 %all-reduce.3.cloned.1.call-done = (f32[32,256]{1,0:T(8,128)}, f32[40,256]{1,0:T(8,128)}) async-done(((f32[32,256]{1,0:T(8,128)}, f32[40,256]{1,0:T(8,128)}), (f32[32,256]{1,0:T(8,128)}, f32[40,256]{1,0:T(8,128)})) %all-reduce.3.cloned.1.call-update) | async-done | bytes 73744 | tf_op jit(solution)/shard_map/psum | solution.py:25
  331.6 1.4 copy.23
  332.9 1.4 copy.24
Async XLA Ops:
  9.0 10.4 %copy-start.1 = (f32[40,256]{1,0:T(8,128)S(1)}, f32[40,256]{1,0:T(8,128)}, u32[]{:S(2)}) copy-start(f32[40,256]{1,0:T(8,128)} %param.7) | copy-start | bytes 122884
  9.0 10.4 %copy-start.2 = (f32[32,256]{1,0:T(8,128)S(1)}, f32[32,256]{1,0:T(8,128)}, u32[]{:S(2)}) copy-start(f32[32,256]{1,0:T(8,128)} %param.6) | copy-start | bytes 98308
  9.0 37.8 %all-to-all-start = ((f32[32,32,256]{2,1,0:T(8,128)}), f32[32,32,256]{2,1,0:T(8,128)S(1)}, u32[]{:S(2)}, u32[]{:S(2)}) async-start(f32[32,32,256]{2,1,0:T(8,128)} %stack.2), calls=%async_computation | async-start | bytes 2097152 | tf_op jit(solution)/shard_map/all_to_all | solution.py:15
  19.4 170.0 %reduce-scatter.2.cloned.1.call-start = ((), (), s32[]{:S(2)}) async-start(), calls=%async_computation.2 | async-start | bytes 1081344 | tf_op jit(solution)/shard_map/reduce_scatter | solution.py:26
  53.5 2.3 copy-start
  65.4 266.2 %all-reduce.3.cloned.1.call-start = ((), (), s32[]{:S(2)}) async-start(), calls=%async_computation.3 | async-start | bytes 147456 | tf_op jit(solution)/shard_map/psum | solution.py:25
Sparse Core Ops, SparseCore 0:
  65.5 123.8 reduce-scatter.1
  192.9 138.5 all-reduce.2
